TPU v7x, 32 devices: a whole 2x2x4 slice. The times are simulated.
32 devices in a mesh: dp: 8 (over z, x), tensor: 4 (over y, core).
Axes of the slice: x: 2, y: 2, z: 4, core: 2. Of those that a mesh axis runs over, the one named last changes fastest.
Arguments:
- layer_input: bfloat16 [8192, 2048], P(('dp', 'tensor')), may hold values from -6 to 6
- segments: int32 [8192], P('dp'), may hold values from 0 to 8191, as said below
- positions: int32 [8192], P('dp'), may hold values from 0 to 1023, as said below
- first_gain: bfloat16 [2048], P('dp'), may hold values from 0.5 to 1.5
- first_shift: bfloat16 [2048], P('dp'), may hold values from -4 to 4
- query_weight: bfloat16 [2048, 2048], P('dp', 'tensor'), may hold values from -0.125 to 0.125
- key_weight: bfloat16 [2048, 2048], P('dp', 'tensor'), may hold values from -0.125 to 0.125
- value_weight: bfloat16 [2048, 2048], P('dp', 'tensor'), may hold values from -0.125 to 0.125
- query_bias: bfloat16 [32, 64], P('tensor', 'dp'), may hold values from -6 to 6
- key_bias: bfloat16 [32, 16], P('tensor'), may hold values from -6 to 6
- value_bias: bfloat16 [32, 64], P('tensor', 'dp'), may hold values from -6 to 6
- out_weight: bfloat16 [2048, 2048], P('tensor', 'dp'), may hold values from -0.5 to 0.5
- second_gain: bfloat16 [2048], P('dp'), may hold values from 0.5 to 1.5
- second_shift: bfloat16 [2048], P('dp'), may hold values from -4 to 4
- gate_weight: bfloat16 [2048, 5632], P('dp', 'tensor'), may hold values from -0.125 to 0.125
- up_weight: bfloat16 [2048, 5632], P('dp', 'tensor'), may hold values from -0.125 to 0.125
- down_weight: bfloat16 [5632, 2048], P('tensor', 'dp'), may hold values from -0.078125 to 0.078125
- out_grad: bfloat16 [8192, 2048], P(('dp', 'tensor')), may hold values from -6 to 6
Outputs:
- layer_output: bfloat16 [8192, 2048], P(('dp', 'tensor'))
- input_grad: float32 [8192, 2048], P(('dp', 'tensor'))
- first_gain_grad: float32 [2048], P(('dp', 'tensor'))
- first_shift_grad: float32 [2048], P(('dp', 'tensor'))
- query_weight_grad: float32 [2048, 2048], P('dp', 'tensor')
- key_weight_grad: float32 [2048, 2048], P('dp', 'tensor')
- value_weight_grad: float32 [2048, 2048], P('dp', 'tensor')
- query_bias_grad: float32 [32, 64], P('tensor', 'dp')
- key_bias_grad: float32 [32, 16], P('tensor')
- value_bias_grad: float32 [32, 64], P('tensor', 'dp')
- out_weight_grad: float32 [2048, 2048], P('tensor', 'dp')
- second_gain_grad: float32 [2048], P(('dp', 'tensor'))
- second_shift_grad: float32 [2048], P(('dp', 'tensor'))
- gate_weight_grad: float32 [2048, 5632], P('dp', 'tensor')
- up_weight_grad: float32 [2048, 5632], P('dp', 'tensor')
- down_weight_grad: float32 [5632, 2048], P('tensor', 'dp')
Inputs may be any that keep to these rules, and one draw needn't show every extreme that they name: `segments`: the tokens form runs of 1024 rows that start at multiples of 1024; the first token of each run starts a new segment. A token's segment number is the row index of the last token of its segment, so numbers never fall along the rows and no two runs share one. `positions`: each token's position counts the earlier tokens of its segment.
All inputs are finite; a program needn't handle non-finite values.
Results may differ from a plain program's by a relative error of at most 0.015.
Values may be sent and summed in bfloat16 or wider, within the bound.
A program may use at most 256 MiB of HBM per device.

v0:
```python
import math
import jax
import jax.numpy as jnp
from jax import lax
from jax.sharding import PartitionSpec as P

HD = 64
ROT = 16
SEQ = 1024
EPS = 1e-05
NEG = -1e30


def rope_angles(positions):
    half = ROT // 2
    freqs = jnp.exp(-(2.0 / ROT) * jnp.arange(half).astype(jnp.float32) * math.log(10000.0))
    return positions.astype(jnp.float32)[:, None] * freqs[None, :]


def turn(heads, cosine, sine, direction):
    half = ROT // 2
    first = heads[..., :half]
    second = heads[..., half:ROT]
    return jnp.concatenate(
        [
            first * cosine - direction * second * sine,
            second * cosine + direction * first * sine,
            heads[..., ROT:],
        ],
        axis=-1,
    )


def norm_forward(rows, gain, shift):
    center = rows - jnp.mean(rows, axis=-1, keepdims=True)
    rstd = lax.rsqrt(jnp.mean(center * center, axis=-1, keepdims=True) + EPS)
    normal = center * rstd
    return (normal, rstd, normal * gain + shift)


def norm_backward(grad_out, normal, rstd, gain):
    scaled = grad_out * gain
    return rstd * (
        scaled
        - jnp.mean(scaled, axis=-1, keepdims=True)
        - normal * jnp.mean(scaled * normal, axis=-1, keepdims=True)
    )


def allowed_pairs(segments, start, base, block):
    q_index = start + jnp.arange(block, dtype=jnp.int32)
    k_index = base + jnp.arange(SEQ, dtype=jnp.int32)
    q_segs = lax.dynamic_slice_in_dim(segments, start, block, 0)
    return (k_index[None, :] <= q_index[:, None]) & (segments[None, :] == q_segs[:, None])


def block_scores(q_rot, k_rot, segments, number, block):
    start = number * block
    base = start // SEQ * SEQ
    q_part = lax.dynamic_slice_in_dim(q_rot, start, block, 0)
    raw = jnp.einsum("qhd,khd->hqk", q_part, k_rot, preferred_element_type=jnp.float32)
    allowed = allowed_pairs(segments, start, base, block)
    scores = jnp.where(allowed[None], raw * HD ** (-0.5), NEG)
    return (scores, start, base, q_part, k_rot)


def attend_forward(q_rot, k_rot, v_heads, segments):
    block = min(512, SEQ)
    count = q_rot.shape[0] // block

    def one_block(number):
        scores, start, base, q_part, k_part = block_scores(q_rot, k_rot, segments, number, block)
        top = jnp.max(scores, axis=-1, keepdims=True)
        expo = jnp.exp(scores - top)
        total = jnp.sum(expo, axis=-1, keepdims=True)
        probs = (expo / total).astype(jnp.bfloat16)
        mixed = jnp.einsum("hqk,khd->qhd", probs, v_heads, preferred_element_type=jnp.float32)
        return (mixed, (top + jnp.log(total))[..., 0])

    mixed, log_sums = lax.map(one_block, jnp.arange(count, dtype=jnp.int32))
    return (mixed.reshape(q_rot.shape), log_sums)


def attend_backward(q_rot, k_rot, v_heads, segments, log_sums, grad_mixed):
    block = min(512, SEQ)
    count = q_rot.shape[0] // block
    start_acc = (jnp.zeros(k_rot.shape, jnp.float32), jnp.zeros(v_heads.shape, jnp.float32))

    def one_block(carry, item):
        key_acc, value_acc = carry
        number, log_part = item
        scores, start, base, q_part, k_part = block_scores(q_rot, k_rot, segments, number, block)
        grad_part = lax.dynamic_slice_in_dim(grad_mixed, start, block, 0)
        probs = jnp.exp(scores - log_part[..., None])
        grad_probs = jnp.einsum(
            "qhd,khd->hqk", grad_part, v_heads, preferred_element_type=jnp.float32
        )
        inner = jnp.sum(probs * grad_probs, axis=-1, keepdims=True)
        grad_scores = (probs * (grad_probs - inner) * HD ** (-0.5)).astype(jnp.bfloat16)
        q_grad = jnp.einsum("hqk,khd->qhd", grad_scores, k_part, preferred_element_type=jnp.float32)
        k_grad = jnp.einsum("hqk,qhd->khd", grad_scores, q_part, preferred_element_type=jnp.float32)
        v_grad = jnp.einsum(
            "hqk,qhd->khd",
            probs.astype(jnp.bfloat16),
            grad_part,
            preferred_element_type=jnp.float32,
        )
        key_acc = key_acc + k_grad
        value_acc = value_acc + v_grad
        return ((key_acc, value_acc), q_grad)

    (key_acc, value_acc), q_blocks = lax.scan(
        one_block, start_acc, (jnp.arange(count, dtype=jnp.int32), log_sums)
    )
    return (q_blocks.reshape(q_rot.shape), key_acc, value_acc)


def local(
    layer_input,
    segments,
    positions,
    first_gain,
    first_shift,
    query_weight,
    key_weight,
    value_weight,
    query_bias,
    key_bias,
    value_bias,
    out_weight,
    second_gain,
    second_shift,
    gate_weight,
    up_weight,
    down_weight,
    out_grad,
):
    f32 = jnp.float32
    bf16 = jnp.bfloat16
    query_full, key_full, value_full, out_full, bias_query, bias_value, gain_one, shift_one = (
        lax.all_gather(query_weight, "dp", axis=0, tiled=True),
        lax.all_gather(key_weight, "dp", axis=0, tiled=True),
        lax.all_gather(value_weight, "dp", axis=0, tiled=True),
        lax.all_gather(out_weight, "dp", axis=1, tiled=True),
        lax.all_gather(query_bias, "dp", axis=1, tiled=True),
        lax.all_gather(value_bias, "dp", axis=1, tiled=True),
        lax.all_gather(first_gain, "dp", axis=0, tiled=True),
        lax.all_gather(first_shift, "dp", axis=0, tiled=True),
    )
    gate_full, up_full, down_full, gain_two, shift_two = (
        lax.all_gather(gate_weight, "dp", axis=0, tiled=True),
        lax.all_gather(up_weight, "dp", axis=0, tiled=True),
        lax.all_gather(down_weight, "dp", axis=1, tiled=True),
        lax.all_gather(second_gain, "dp", axis=0, tiled=True),
        lax.all_gather(second_shift, "dp", axis=0, tiled=True),
    )
    rows = layer_input.astype(f32)
    gain_one_f = gain_one.astype(f32)
    hat_one, rstd_one, normed_one = norm_forward(rows, gain_one_f, shift_one.astype(f32))
    norm_one_full = lax.all_gather(normed_one.astype(bf16), "tensor", axis=0, tiled=True)
    total_rows = norm_one_full.shape[0]
    local_heads = query_full.shape[1] // HD
    bias_key_full = jnp.pad(key_bias.astype(f32), ((0, 0), (0, HD - ROT))).reshape(-1)
    q_lin = jnp.dot(norm_one_full, query_full, preferred_element_type=f32) + bias_query.astype(
        f32
    ).reshape(-1)
    k_lin = jnp.dot(norm_one_full, key_full, preferred_element_type=f32) + bias_key_full
    v_lin = jnp.dot(norm_one_full, value_full, preferred_element_type=f32) + bias_value.astype(
        f32
    ).reshape(-1)
    angles = rope_angles(positions)
    cosine = jnp.cos(angles)[:, None, :]
    sine = jnp.sin(angles)[:, None, :]
    q_rot = turn(q_lin.reshape(total_rows, local_heads, HD), cosine, sine, 1.0).astype(bf16)
    k_rot = turn(k_lin.reshape(total_rows, local_heads, HD), cosine, sine, 1.0).astype(bf16)
    v_heads = v_lin.reshape(total_rows, local_heads, HD).astype(bf16)
    mixed, log_sums = attend_forward(q_rot, k_rot, v_heads, segments)
    mixed_low = mixed.reshape(total_rows, -1).astype(bf16)
    attended = rows + lax.psum_scatter(
        jnp.dot(mixed_low, out_full, preferred_element_type=f32),
        "tensor",
        scatter_dimension=0,
        tiled=True,
    )
    gain_two_f = gain_two.astype(f32)
    hat_two, rstd_two, normed_two = norm_forward(attended, gain_two_f, shift_two.astype(f32))
    norm_two_full = lax.all_gather(normed_two.astype(bf16), "tensor", axis=0, tiled=True)
    gate_lin = jnp.dot(norm_two_full, gate_full, preferred_element_type=f32)
    up_lin = jnp.dot(norm_two_full, up_full, preferred_element_type=f32)
    sigma = jax.nn.sigmoid(gate_lin)
    activated = gate_lin * sigma
    hidden_low = (activated * up_lin).astype(bf16)
    layer_output = (
        attended
        + lax.psum_scatter(
            jnp.dot(hidden_low, down_full, preferred_element_type=f32).astype(jnp.bfloat16),
            "tensor",
            scatter_dimension=0,
            tiled=True,
        ).astype(jnp.float32)
    ).astype(bf16)
    fresh = (
        lax.all_gather(query_weight, "dp", axis=0, tiled=True),
        lax.all_gather(key_weight, "dp", axis=0, tiled=True),
        lax.all_gather(value_weight, "dp", axis=0, tiled=True),
        lax.all_gather(out_weight, "dp", axis=1, tiled=True),
        lax.all_gather(gate_weight, "dp", axis=0, tiled=True),
        lax.all_gather(up_weight, "dp", axis=0, tiled=True),
        lax.all_gather(down_weight, "dp", axis=1, tiled=True),
        lax.all_gather(second_gain, "dp", axis=0, tiled=True),
    )
    query_back, key_back, value_back, out_back, gate_back, up_back, down_back, gain_back = fresh
    grad_full = lax.all_gather(out_grad, "tensor", axis=0, tiled=True)
    grad_hidden = jnp.einsum("sd,fd->sf", grad_full, down_back, preferred_element_type=f32)
    down_grad = jnp.einsum("sf,sd->fd", hidden_low, grad_full, preferred_element_type=f32)
    grad_gate = (grad_hidden * up_lin * sigma * (1.0 + gate_lin * (1.0 - sigma))).astype(bf16)
    grad_up = (grad_hidden * activated).astype(bf16)
    gate_grad = jnp.einsum("sd,sf->df", norm_two_full, grad_gate, preferred_element_type=f32)
    up_grad = jnp.einsum("sd,sf->df", norm_two_full, grad_up, preferred_element_type=f32)
    grad_norm_two = lax.psum_scatter(
        jnp.einsum("sf,df->sd", grad_gate, gate_back, preferred_element_type=f32)
        + jnp.einsum("sf,df->sd", grad_up, up_back, preferred_element_type=f32),
        "tensor",
        scatter_dimension=0,
        tiled=True,
    )
    gain_two_grad = jnp.sum(grad_norm_two * hat_two, axis=0)
    shift_two_grad = jnp.sum(grad_norm_two, axis=0)
    grad_attended = out_grad.astype(f32) + norm_backward(
        grad_norm_two, hat_two, rstd_two, gain_back.astype(f32)
    )
    residual_full = lax.all_gather(grad_attended.astype(bf16), "tensor", axis=0, tiled=True)
    grad_mixed = jnp.einsum(
        "sd,kd->sk", residual_full, out_back, preferred_element_type=f32
    ).astype(bf16)
    out_weight_grad = jnp.einsum("sk,sd->kd", mixed_low, residual_full, preferred_element_type=f32)
    grad_qrot, grad_krot, grad_vheads = attend_backward(
        q_rot, k_rot, v_heads, segments, log_sums, grad_mixed.reshape(total_rows, local_heads, HD)
    )
    grad_query = turn(grad_qrot, cosine, sine, -1.0).reshape(total_rows, -1)
    grad_key = turn(grad_krot, cosine, sine, -1.0).reshape(total_rows, -1)
    grad_value = grad_vheads.reshape(total_rows, -1)
    query_bias_grad = jnp.sum(grad_query, axis=0).reshape(local_heads, HD)
    key_bias_grad = jnp.sum(grad_key, axis=0).reshape(local_heads, HD)[:, :ROT]
    value_bias_grad = jnp.sum(grad_value, axis=0).reshape(local_heads, HD)
    query_low = grad_query.astype(bf16)
    key_low = grad_key.astype(bf16)
    value_low = grad_value.astype(bf16)
    query_weight_grad = jnp.einsum(
        "sd,sk->dk", norm_one_full, query_low, preferred_element_type=f32
    )
    key_weight_grad = jnp.einsum("sd,sk->dk", norm_one_full, key_low, preferred_element_type=f32)
    value_weight_grad = jnp.einsum(
        "sd,sk->dk", norm_one_full, value_low, preferred_element_type=f32
    )
    total = jnp.einsum("sk,dk->sd", query_low, query_back, preferred_element_type=f32)
    total = total + jnp.einsum("sk,dk->sd", key_low, key_back, preferred_element_type=f32)
    grad_norm_one = lax.psum_scatter(
        total + jnp.einsum("sk,dk->sd", value_low, value_back, preferred_element_type=f32),
        "tensor",
        scatter_dimension=0,
        tiled=True,
    )
    gain_one_grad = jnp.sum(grad_norm_one * hat_one, axis=0)
    shift_one_grad = jnp.sum(grad_norm_one, axis=0)
    input_grad = grad_attended + norm_backward(grad_norm_one, hat_one, rstd_one, gain_one_f)
    gate_sum, up_sum, down_sum = (
        lax.psum_scatter(gate_grad, "dp", scatter_dimension=0, tiled=True),
        lax.psum_scatter(up_grad, "dp", scatter_dimension=0, tiled=True),
        lax.psum_scatter(down_grad, "dp", scatter_dimension=1, tiled=True),
    )
    query_sum, key_sum, value_sum, out_sum, bquery_sum, bvalue_sum = (
        lax.psum_scatter(query_weight_grad, "dp", scatter_dimension=0, tiled=True),
        lax.psum_scatter(key_weight_grad, "dp", scatter_dimension=0, tiled=True),
        lax.psum_scatter(value_weight_grad, "dp", scatter_dimension=0, tiled=True),
        lax.psum_scatter(out_weight_grad, "dp", scatter_dimension=1, tiled=True),
        lax.psum_scatter(query_bias_grad, "dp", scatter_dimension=1, tiled=True),
        lax.psum_scatter(value_bias_grad, "dp", scatter_dimension=1, tiled=True),
    )
    bkey_sum = lax.psum(key_bias_grad, "dp")
    gain_one_sum, shift_one_sum, gain_two_sum, shift_two_sum = (
        lax.psum_scatter(gain_one_grad, ("dp", "tensor"), scatter_dimension=0, tiled=True),
        lax.psum_scatter(shift_one_grad, ("dp", "tensor"), scatter_dimension=0, tiled=True),
        lax.psum_scatter(gain_two_grad, ("dp", "tensor"), scatter_dimension=0, tiled=True),
        lax.psum_scatter(shift_two_grad, ("dp", "tensor"), scatter_dimension=0, tiled=True),
    )
    return (
        layer_output,
        input_grad,
        gain_one_sum,
        shift_one_sum,
        query_sum,
        key_sum,
        value_sum,
        bquery_sum,
        bkey_sum,
        bvalue_sum,
        out_sum,
        gain_two_sum,
        shift_two_sum,
        gate_sum,
        up_sum,
        down_sum,
    )


def solution(mesh):
    return jax.shard_map(
        local,
        mesh=mesh,
        in_specs=(
            P(("dp", "tensor"), None),
            P("dp"),
            P("dp"),
            P("dp"),
            P("dp"),
            P("dp", "tensor"),
            P("dp", "tensor"),
            P("dp", "tensor"),
            P("tensor", "dp"),
            P("tensor", None),
            P("tensor", "dp"),
            P("tensor", "dp"),
            P("dp"),
            P("dp"),
            P("dp", "tensor"),
            P("dp", "tensor"),
            P("tensor", "dp"),
            P(("dp", "tensor"), None),
        ),
        out_specs=(
            P(("dp", "tensor"), None),
            P(("dp", "tensor"), None),
            P(("dp", "tensor")),
            P(("dp", "tensor")),
            P("dp", "tensor"),
            P("dp", "tensor"),
            P("dp", "tensor"),
            P("tensor", "dp"),
            P("tensor", None),
            P("tensor", "dp"),
            P("tensor", "dp"),
            P(("dp", "tensor")),
            P(("dp", "tensor")),
            P("dp", "tensor"),
            P("dp", "tensor"),
            P("tensor", "dp"),
        ),
        check_vma=False,
    )
```

profile of v0, /device:TPU:0, one launch (start us, length us, event | category | flops | bytes accessed | tf_op | source)
XLA Modules:
  0.0 2123.0 jit_solution(928444203976927270)
XLA Ops:
  9.3 22.2 %all-gather.1 = bf16[8,1,256]{2,1,0:T(2,128)(2,1)S(1)} all-gather(bf16[1,1,256]{2,1,0:T(2,128)(2,1)S(1)} %reshape.335), channel_id=1, replica_groups=mesh['dp'=8,'tensor'=4] {'dp'}, dimensions={0}, use_global_device_ids=true | all-gather | bytes 4608 | tf_op jit(solution)/shard_map/all_gather | solution.py:148
  31.5 16.4 all-gather
  55.5 26.0 %all_gather.66 = bf16[8,64]{0,1:T(8,128)(2,1)S(1)} all-gather(bf16[8,8]{0,1:T(8,128)(2,1)S(1)} %copy.48), channel_id=1, replica_groups=mesh['dp'=8,'tensor'=4] {'dp'}, dimensions={1}, use_global_device_ids=true | all-gather | bytes 1152 | tf_op jit(solution)/shard_map/all_gather | solution.py:146
  81.6 26.0 %all_gather.63 = bf16[8,64]{0,1:T(8,128)(2,1)S(1)} all-gather(bf16[8,8]{0,1:T(8,128)(2,1)S(1)} %copy.46), channel_id=1, replica_groups=mesh['dp'=8,'tensor'=4] {'dp'}, dimensions={1}, use_global_device_ids=true | all-gather | bytes 1152 | tf_op jit(solution)/shard_map/all_gather | solution.py:145
  108.6 5.2 convolution_add_fusion.1
  115.3 33.6 %all-gather.18.cloned.1.call-done = bf16[2048,512]{1,0:T(8,128)(2,1)} async-done(((bf16[256,512]{1,0:T(8,128)(2,1)}), bf16[2048,512]{1,0:T(8,128)(2,1)}) %all-gather.18.cloned.1.call-update) | async-done | bytes 2097168 | tf_op jit(solution)/shard_map/all_gather | solution.py:141
  148.9 5.2 convolution_add_fusion.2
  157.0 41.7 %all-gather.22.cloned.1.call-done = bf16[2048,512]{1,0:T(8,128)(2,1)} async-done(((bf16[256,512]{1,0:T(8,128)(2,1)}), bf16[2048,512]{1,0:T(8,128)(2,1)}) %all-gather.22.cloned.1.call-update) | async-done | bytes 2097168 | tf_op jit(solution)/shard_map/all_gather | solution.py:143
  198.7 6.2 add_convert_fusion.2
  204.9 34.0 %while.31 = (s32[]{:T(128)}, bf16[2,512,8,64]{1,3,2,0:T(8,128)(2,1)S(1)}, f32[2,8,512]{2,1,0:T(8,128)S(1)}, s32[2]{0:T(128)S(1)}, s32[1024]{0:T(1024)S(1)}, /*in...) while((s32[]{:T(128)}, ...), condition=%wide.region_5.6_spmd, body=%wide.region_2.5_spmd.sunk | while | flops 1125643776 | bytes 56252800 | solution.py:80
  206.9 4.9 fusion.145
  216.1 5.9 fusion.147
  223.9 4.9 fusion.145
  228.7 4.2 fusion.146
  233.0 5.9 fusion.147
  240.3 10.0 all-gather.24.cloned.1.call-done
  250.2 7.2 fusion.66
  258.4 17.7 all-gather.3
  276.1 16.9 all-gather.2
  292.9 34.6 %reduce-scatter.14.cloned.1.call-done = f32[256,2048]{1,0:T(8,128)} async-done(((f32[1024,2048]{1,0:T(8,128)}), f32[256,2048]{1,0:T(8,128)}) %reduce-scatter.14.cloned.1.call-update) | async-done | bytes 2097168 | tf_op jit(solution)/shard_map/reduce_scatter | solution.py:179
  333.4 89.3 %all-gather.30.cloned.1.call-done = bf16[2048,1408]{1,0:T(8,128)(2,1)} async-done(((bf16[256,1408]{1,0:T(8,128)(2,1)}), bf16[2048,1408]{1,0:T(8,128)(2,1)}) %all-gather.30.cloned.1.call-update) | async-done | bytes 5767184 | tf_op jit(solution)/shard_map/all_gather | solution.py:152
  422.6 34.9 %all-gather.26.cloned.1.call-done = bf16[1024,2048]{1,0:T(8,128)(2,1)} async-done(((bf16[256,2048]{1,0:T(8,128)(2,1)}), bf16[1024,2048]{1,0:T(8,128)(2,1)}) %all-gather.26.cloned.1.call-update) | async-done | bytes 4194320 | tf_op jit(solution)/shard_map/all_gather | solution.py:187
  457.6 11.9 fusion.68
  469.5 83.2 %all-gather.28.cloned.1.call-done = bf16[2048,1408]{1,0:T(8,128)(2,1)} async-done(((bf16[256,1408]{1,0:T(8,128)(2,1)}), bf16[2048,1408]{1,0:T(8,128)(2,1)}) %all-gather.28.cloned.1.call-update) | async-done | bytes 5767184 | tf_op jit(solution)/shard_map/all_gather | solution.py:151
  552.7 11.7 fusion.67
  564.4 22.5 %all-gather.34.cloned.1.call-done = bf16[1024,2048]{1,0:T(8,128)(2,1)} async-done(((bf16[256,2048]{1,0:T(8,128)(2,1)}), bf16[1024,2048]{1,0:T(8,128)(2,1)}) %all-gather.34.cloned.1.call-update) | async-done | bytes 4194320 | tf_op jit(solution)/shard_map/all_gather | solution.py:213
  586.8 95.9 %all-gather.32.cloned.1.call-done = bf16[1408,2048]{1,0:T(8,128)(2,1)} async-done(((bf16[1408,256]{1,0:T(8,128)(2,1)}), bf16[1408,2048]{1,0:T(8,128)(2,1)}) %all-gather.32.cloned.1.call-update) | async-done | bytes 5767184 | tf_op jit(solution)/shard_map/all_gather | solution.py:153
  682.7 16.6 multiply_convert_fusion.1
  699.4 8.7 fusion.69
  708.0 11.3 convolution_add_fusion
  719.4 10.9 convolution_convert_fusion
  730.4 59.0 %reduce-scatter.18.cloned.1.call-done = f32[256,2048]{1,0:T(8,128)} async-done(((f32[1024,2048]{1,0:T(8,128)}), f32[256,2048]{1,0:T(8,128)}) %reduce-scatter.18.cloned.1.call-update) | async-done | bytes 2097168 | tf_op jit(solution)/shard_map/reduce_scatter | solution.py:220
  792.5 44.0 %reduce-scatter.16.cloned.1.call-done = bf16[256,2048]{1,0:T(8,128)(2,1)} async-done(((bf16[1024,2048]{1,0:T(8,128)(2,1)}), bf16[256,2048]{1,0:T(8,128)(2,1)}) %reduce-scatter.16.cloned.1.call-update) | async-done | bytes 1048592 | tf_op jit(solution)/shard_map/reduce_scatter | solution.py:195
  836.5 5.0 fusion.63
  841.6 34.6 %all-gather.36.cloned.1.call-done = bf16[1024,2048]{1,0:T(8,128)(2,1)} async-done(((bf16[256,2048]{1,0:T(8,128)(2,1)}), bf16[1024,2048]{1,0:T(8,128)(2,1)}) %all-gather.36.cloned.1.call-update) | async-done | bytes 4194320 | tf_op jit(solution)/shard_map/all_gather | solution.py:232
  876.2 6.2 convolution_convert_fusion.1
  882.4 183.4 %while.32 = (s32[]{:T(128)}, f32[1024,8,64]{0,2,1:T(8,128)}, f32[1024,8,64]{0,2,1:T(8,128)S(1)}, f32[2,512,8,64]{1,0,3,2:T(2,128)}, s32[2]{0:T(128)S(1)}, /*inde...) while((s32[]{:T(128)}, f32[1024,8,64]{0,2,1:T(8,128)}, ...), condition=%wide.region_15.16_spmd.clone, body=%wide.region_13.15_spmd.clone.sunk | while | flops 2746756608 | bytes 238098896 | solution.py:112
  884.4 5.9 subtract_exponential_fusion.3
  896.0 9.5 fusion.158
  905.5 22.9 %fusion.159 = f32[1,512,8,64]{1,3,2,0:T(8,128)} fusion(bf16[1024,8,64]{0,2,1:T(8,128)(2,1)} %get-tuple-element.590, f32[8,512,1024]{2,1,0:T(8,128)} %copy-done, f32[8,512,1024]{2,1,0:T(8,128)} %fusion.158), kind=kOutput, calls=%fused_computation.31.clone.1 | convolution fusion | flops 557847552 | bytes 35651584 | tf_op jit(solution)/shard_map/while/body/eval_jaxpr/hqk,khd->qhd/dot_general | solution.py:100
  928.4 23.5 %bitcast_add_fusion.4 = f32[1024,8,64]{0,2,1:T(8,128)} fusion(f32[1024,8,64]{0,2,1:T(8,128)} %get-tuple-element.566, f32[8,512,1024]{2,1,0:T(8,128)} %copy-done, f32[8,512,1024]{2,1,0:T(8,128)} %fusion.158, pred[]{:T(512)S(6)} %compare.14, bf16[1024,8,64]{0,2,1:T(8,128)(2,1)} %get-tuple-element.588, s32[]{:T(128)S(6)} %select_n.75), kind=kOutput, calls=%fused_computation.29.clone.1 | convolution fusion | flops 558896128 | bytes 71827464 | tf_op jit(solution)/shard_map/while/body/eval_jaxpr/hqk,qhd->khd/dot_general | solution.py:101
  954.2 19.6 dynamic_update_slice.28
  975.6 5.9 subtract_exponential_fusion.3
  987.3 9.5 fusion.158
  996.8 22.9 %fusion.159 = f32[1,512,8,64]{1,3,2,0:T(8,128)} fusion(bf16[1024,8,64]{0,2,1:T(8,128)(2,1)} %get-tuple-element.590, f32[8,512,1024]{2,1,0:T(8,128)} %copy-done, f32[8,512,1024]{2,1,0:T(8,128)} %fusion.158), kind=kOutput, calls=%fused_computation.31.clone.1 | convolution fusion | flops 557847552 | bytes 35651584 | tf_op jit(solution)/shard_map/while/body/eval_jaxpr/hqk,khd->qhd/dot_general | solution.py:100
  1019.6 24.0 %bitcast_add_fusion.4 = f32[1024,8,64]{0,2,1:T(8,128)} fusion(f32[1024,8,64]{0,2,1:T(8,128)} %get-tuple-element.566, f32[8,512,1024]{2,1,0:T(8,128)} %copy-done, f32[8,512,1024]{2,1,0:T(8,128)} %fusion.158, pred[]{:T(512)S(6)} %compare.14, bf16[1024,8,64]{0,2,1:T(8,128)(2,1)} %get-tuple-element.588, s32[]{:T(128)S(6)} %select_n.75), kind=kOutput, calls=%fused_computation.29.clone.1 | convolution fusion | flops 558896128 | bytes 71827464 | tf_op jit(solution)/shard_map/while/body/eval_jaxpr/hqk,qhd->khd/dot_general | solution.py:101
  1045.9 19.6 dynamic_update_slice.28
  1080.3 5.8 add_add_fusion
  1086.2 12.3 fusion.78
  1098.5 13.0 fusion.77
  1111.6 11.9 fusion.76
  1123.6 7.1 fusion.75
  1130.7 6.7 fusion.74
  1137.6 6.6 fusion.73
  1144.2 6.6 fusion.72
  1154.6 38.4 %all-reduce.8 = (f32[8,64]{1,0:T(8,128)S(1)}, f32[8,16]{1,0:T(8,128)}, f32[8,64]{1,0:T(8,128)S(1)}) all-reduce(f32[8,64]{1,0:T(8,128)S(1)} %fusion.61, f32[8,16]{1,0:T(8,128)S(1)} %bitcast.138, f32[8,64]{1,0:T(8,128)S(1)} %get-tuple-element.370), channel_id=11, replica_groups=mesh['dp'=8,'tensor'=4] {'dp'}, use_global_device_ids=true, to_apply=%region_27.28.clone | all-reduce | flops 1152 | bytes 9216
  1197.0 41.2 %all-reduce.7 = (f32[2048]{0:T(1024)S(1)}, f32[2048]{0:T(1024)S(1)}, f32[2048]{0:T(1024)S(1)}, f32[2048]{0:T(1024)S(1)}) all-reduce(f32[2048]{0:T(1024)S(1)} %get-tuple-element.302, f32[2048]{0:T(1024)S(1)} %get-tuple-element.307, f32[2048]{0:T(1024)S(1)} %copy-done.24, ...), channel_id=6, replica_groups=mesh['dp'=8,'tensor'=4] {'dp','tensor'}, use_global_device_ids=true, to_apply=%region_20.21.clone | all-reduce | flops 8192 | bytes 65536
  1244.3 112.0 %reduce-scatter.34.cloned.1.call-done = f32[1408,256]{1,0:T(8,128)} async-done(((f32[1408,2048]{1,0:T(8,128)}), f32[1408,256]{1,0:T(8,128)}) %reduce-scatter.34.cloned.1.call-update) | async-done | bytes 1441808 | tf_op jit(solution)/shard_map/reduce_scatter | solution.py:270
  1356.3 195.9 %reduce-scatter.32.cloned.1.call-done = f32[256,1408]{1,0:T(8,128)} async-done(((f32[2048,1408]{1,0:T(8,128)}), f32[256,1408]{1,0:T(8,128)}) %reduce-scatter.32.cloned.1.call-update) | async-done | bytes 1441808 | tf_op jit(solution)/shard_map/reduce_scatter | solution.py:269
  1552.1 195.9 %reduce-scatter.30.cloned.1.call-done = f32[256,1408]{1,0:T(8,128)} async-done(((f32[2048,1408]{1,0:T(8,128)}), f32[256,1408]{1,0:T(8,128)}) %reduce-scatter.30.cloned.1.call-update) | async-done | bytes 1441808 | tf_op jit(solution)/shard_map/reduce_scatter | solution.py:268
  1748.0 91.6 %reduce-scatter.28.cloned.1.call-done = f32[512,256]{1,0:T(8,128)} async-done(((f32[512,2048]{1,0:T(8,128)}), f32[512,256]{1,0:T(8,128)}) %reduce-scatter.28.cloned.1.call-update) | async-done | bytes 524304 | tf_op jit(solution)/shard_map/reduce_scatter | solution.py:276
  1839.7 92.2 %reduce-scatter.26.cloned.1.call-done = f32[256,512]{1,0:T(8,128)} async-done(((f32[2048,512]{1,0:T(8,128)}), f32[256,512]{1,0:T(8,128)}) %reduce-scatter.26.cloned.1.call-update) | async-done | bytes 524304 | tf_op jit(solution)/shard_map/reduce_scatter | solution.py:275
  1931.8 91.9 %reduce-scatter.24.cloned.1.call-done = f32[256,512]{1,0:T(8,128)} async-done(((f32[2048,512]{1,0:T(8,128)}), f32[256,512]{1,0:T(8,128)}) %reduce-scatter.24.cloned.1.call-update) | async-done | bytes 524304 | tf_op jit(solution)/shard_map/reduce_scatter | solution.py:274
  2023.7 92.3 %reduce-scatter.22.cloned.1.call-done = f32[256,512]{1,0:T(8,128)} async-done(((f32[2048,512]{1,0:T(8,128)}), f32[256,512]{1,0:T(8,128)}) %reduce-scatter.22.cloned.1.call-update) | async-done | bytes 524304 | tf_op jit(solution)/shard_map/reduce_scatter | solution.py:273
  (227 shorter events, 79.0 us)
Async XLA Ops:
  7.2 44.6 %copy-start.1 = (bf16[256,2048]{1,0:T(8,128)(2,1)S(1)}, bf16[256,2048]{1,0:T(8,128)(2,1)}, u32[]{:S(2)}) copy-start(bf16[256,2048]{1,0:T(8,128)(2,1)} %param.22) | copy-start | bytes 3145732
  7.2 101.4 %all-gather.20.cloned.1.call-start = ((), (), s32[]{:S(2)}) async-start(), calls=%async_computation.13 | async-start | bytes 2359296 | tf_op jit(solution)/shard_map/all_gather | solution.py:142
  7.9 100.7 %all-gather.16.cloned.1.call-start = ((), (), s32[]{:S(2)}) async-start(), calls=%async_computation.11 | async-start | bytes 5242880 | tf_op jit(solution)/shard_map/all_gather | solution.py:160
  48.0 3.2 copy-start.22
  48.0 7.2 copy-start.32
  48.0 7.3 copy-start.33
  48.0 7.4 copy-start.30
  48.0 7.4 copy-start.31
  49.5 1.7 copy-start.26
  51.2 0.6 copy-start.28
  53.2 95.7 %all-gather.18.cloned.1.call-start = ((), (), s32[]{:S(2)}) async-start(), calls=%async_computation.12 | async-start | bytes 2359296 | tf_op jit(solution)/shard_map/all_gather | solution.py:141
  53.9 144.8 %all-gather.22.cloned.1.call-start = ((), (), s32[]{:S(2)}) async-start(), calls=%async_computation.14 | async-start | bytes 2359296 | tf_op jit(solution)/shard_map/all_gather | solution.py:143
  54.5 195.7 %all-gather.24.cloned.1.call-start = ((), (), s32[]{:S(2)}) async-start(), calls=%async_computation.15 | async-start | bytes 2359296 | tf_op jit(solution)/shard_map/all_gather | solution.py:144
  55.1 272.5 %reduce-scatter.14.cloned.1.call-start = ((), (), s32[]{:S(2)}) async-start(), calls=%async_computation.16 | async-start | bytes 10485760 | tf_op jit(solution)/shard_map/reduce_scatter | solution.py:179
  108.6 45.7 %copy-start.19 = (f32[1024,8]{0,1:T(8,128)}, f32[1024,8]{0,1:T(8,128)S(1)}, u32[]{:S(2)}) copy-start(f32[1024,8]{0,1:T(8,128)S(1)} %get-tuple-element.379) | copy-start | bytes 98308
  113.9 1.3 copy-start.18
  157.0 47.9 %copy-start.17 = (s32[1024]{0:T(1024)S(1)}, s32[1024]{0:T(1024)}, u32[]{:S(2)}) copy-start(s32[1024]{0:T(1024)} %param.23) | copy-start | bytes 12292
  240.2 17.2 copy-start.16
  257.5 0.8 copy-start.37
  257.5 0.9 copy-start.38
  257.5 70.1 %copy-start.2 = (bf16[256,2048]{1,0:T(8,128)(2,1)S(1)}, bf16[256,2048]{1,0:T(8,128)(2,1)}, u32[]{:S(2)}) copy-start(bf16[256,2048]{1,0:T(8,128)(2,1)} %param.22) | copy-start | bytes 3145732
  257.5 165.1 %all-gather.30.cloned.1.call-start = ((), (), s32[]{:S(2)}) async-start(), calls=%async_computation.19 | async-start | bytes 6488064 | tf_op jit(solution)/shard_map/all_gather | solution.py:152
  258.3 199.3 %all-gather.26.cloned.1.call-start = ((), (), s32[]{:S(2)}) async-start(), calls=%async_computation.17 | async-start | bytes 5242880 | tf_op jit(solution)/shard_map/all_gather | solution.py:187
  331.3 221.4 %all-gather.28.cloned.1.call-start = ((), (), s32[]{:S(2)}) async-start(), calls=%async_computation.18 | async-start | bytes 6488064 | tf_op jit(solution)/shard_map/all_gather | solution.py:151
  332.0 254.8 %all-gather.34.cloned.1.call-start = ((), (), s32[]{:S(2)}) async-start(), calls=%async_computation.22 | async-start | bytes 5242880 | tf_op jit(solution)/shard_map/all_gather | solution.py:213
  332.6 350.1 %all-gather.32.cloned.1.call-start = ((), (), s32[]{:S(2)}) async-start(), calls=%async_computation.20 | async-start | bytes 6488064 | tf_op jit(solution)/shard_map/all_gather | solution.py:153
  333.3 456.1 %reduce-scatter.18.cloned.1.call-start = ((), (), s32[]{:S(2)}) async-start(), calls=%async_computation.23 | async-start | bytes 10485760 | tf_op jit(solution)/shard_map/reduce_scatter | solution.py:220
  682.7 16.6 copy-start.34
  699.4 8.7 copy-start.40
  719.3 117.2 %reduce-scatter.16.cloned.1.call-start = ((), (), s32[]{:S(2)}) async-start(), calls=%async_computation.21 | async-start | bytes 5242880 | tf_op jit(solution)/shard_map/reduce_scatter | solution.py:195
  730.3 106.2 %copy-start.8 = (bf16[256,2048]{1,0:T(8,128)(2,1)S(1)}, bf16[256,2048]{1,0:T(8,128)(2,1)}, u32[]{:S(2)}) copy-start(bf16[256,2048]{1,0:T(8,128)(2,1)} %param.39) | copy-start | bytes 3145732
  730.4 145.8 %all-gather.36.cloned.1.call-start = ((), (), s32[]{:S(2)}) async-start(), calls=%async_computation.24 | async-start | bytes 5242880 | tf_op jit(solution)/shard_map/all_gather | solution.py:232
  841.5 352.8 %reduce-scatter.20.cloned.1.call-start = ((), (), s32[]{:S(2)}) async-start(), calls=%async_computation.25 | async-start | bytes 10485760 | tf_op jit(solution)/shard_map/reduce_scatter | solution.py:258
  890.3 5.7 copy-start
  981.5 5.7 copy-start
  1069.7 2.1 copy-start.15
  1069.7 2.2 copy-start.20
  1069.7 2.3 copy-start.21
  1071.4 3.0 copy-start.4
  1072.0 2.0 copy-start.6
  1073.6 0.7 copy-start.11
  1073.6 0.8 copy-start.13
  1073.6 0.9 copy-start.9
  1073.8 1.6 copy-start.35
  1075.4 2.4 copy-start.36
  1077.9 2.4 copy-start.14
  1086.1 270.2 %reduce-scatter.34.cloned.1.call-start = ((), (), s32[]{:S(2)}) async-start(), calls=%async_computation.32 | async-start | bytes 12976128 | tf_op jit(solution)/shard_map/reduce_scatter | solution.py:270
  1098.4 453.7 %reduce-scatter.32.cloned.1.call-start = ((), (), s32[]{:S(2)}) async-start(), calls=%async_computation.31 | async-start | bytes 12976128 | tf_op jit(solution)/shard_map/reduce_scatter | solution.py:269
  1111.5 636.5 %reduce-scatter.30.cloned.1.call-start = ((), (), s32[]{:S(2)}) async-start(), calls=%async_computation.30 | async-start | bytes 12976128 | tf_op jit(solution)/shard_map/reduce_scatter | solution.py:268
  1123.5 716.1 %reduce-scatter.28.cloned.1.call-start = ((), (), s32[]{:S(2)}) async-start(), calls=%async_computation.29 | async-start | bytes 4718592 | tf_op jit(solution)/shard_map/reduce_scatter | solution.py:276
  1130.6 801.2 %reduce-scatter.26.cloned.1.call-start = ((), (), s32[]{:S(2)}) async-start(), calls=%async_computation.28 | async-start | bytes 4718592 | tf_op jit(solution)/shard_map/reduce_scatter | solution.py:275
  1137.4 886.3 %reduce-scatter.24.cloned.1.call-start = ((), (), s32[]{:S(2)}) async-start(), calls=%async_computation.27 | async-start | bytes 4718592 | tf_op jit(solution)/shard_map/reduce_scatter | solution.py:274
  1144.2 971.8 %reduce-scatter.22.cloned.1.call-start = ((), (), s32[]{:S(2)}) async-start(), calls=%async_computation.26 | async-start | bytes 4718592 | tf_op jit(solution)/shard_map/reduce_scatter | solution.py:273
  1150.8 0.7 copy-start.39
  1150.8 1.9 copy-start.12
  1150.8 3.5 copy-start.5
  1150.8 3.5 copy-start.10
  1150.9 43.4 %copy-start.3 = (bf16[256,2048]{1,0:T(8,128)(2,1)S(1)}, bf16[256,2048]{1,0:T(8,128)(2,1)}, u32[]{:S(2)}) copy-start(bf16[256,2048]{1,0:T(8,128)(2,1)} %param.22) | copy-start | bytes 3145732
  1150.9 43.4 %copy-start.23 = (f32[8,1,256]{2,1,0:T(1,128)S(1)}, f32[8,1,256]{2,1,0:T(1,128)}, u32[]{:S(2)}) copy-start(f32[8,1,256]{2,1,0:T(1,128)} %copy-done.22) | copy-start | bytes 24580
  1150.9 43.4 %copy-start.27 = (f32[256]{0:T(256)S(1)}, f32[256]{0:T(256)}, u32[]{:S(2)}) copy-start(f32[256]{0:T(256)} %copy-done.26) | copy-start | bytes 3076
  1150.9 43.4 %copy-start.29 = (f32[256]{0:T(256)S(1)}, f32[256]{0:T(256)}, u32[]{:S(2)}) copy-start(f32[256]{0:T(256)} %copy-done.28) | copy-start | bytes 3076
  1154.4 42.7 %copy-start.24 = (f32[2048]{0:T(1024)S(1)}, f32[2048]{0:T(1024)}, u32[]{:S(2)}) copy-start(f32[2048]{0:T(1024)} %get-tuple-element.300) | copy-start | bytes 24580
  1154.4 42.7 %copy-start.25 = (f32[2048]{0:T(1024)S(1)}, f32[2048]{0:T(1024)}, u32[]{:S(2)}) copy-start(f32[2048]{0:T(1024)} %get-tuple-element.306) | copy-start | bytes 24580
  1194.3 46.2 %copy-start.7 = (f32[256,2048]{1,0:T(8,128)S(1)}, f32[256,2048]{1,0:T(8,128)}, u32[]{:S(2)}) copy-start(f32[256,2048]{1,0:T(8,128)} %reduce-scatter.20.cloned.1.call-done) | copy-start | bytes 6291460
Sparse Core Ops, SparseCore 0:
  10.2 52.0 all-gather.19
  64.4 33.0 all-gather.15
  99.6 49.2 all-gather.17
  150.9 47.7 all-gather.21
  200.6 49.5 all-gather.23
  257.6 69.8 reduce-scatter.13
  330.0 92.6 all-gather.29
  424.9 32.6 all-gather.25
  460.0 92.6 all-gather.27
  554.1 32.6 all-gather.33
  589.1 93.5 all-gather.31
  719.5 69.9 reduce-scatter.17
  791.9 44.5 reduce-scatter.15
  841.6 34.4 all-gather.35
  1086.2 71.6 reduce-scatter.19
  1162.0 194.2 reduce-scatter.33
  1360.3 191.8 reduce-scatter.31
  1556.2 191.8 reduce-scatter.29
  1752.2 87.3 reduce-scatter.27
  1844.1 87.6 reduce-scatter.25
  1936.0 87.6 reduce-scatter.23
  2028.3 87.6 reduce-scatter.21
where the time goes:
time: 2130 us; the launch traced here: 2120 us
  waiting for transfers between devices  1460 us (69%)
  matrix products  328 us (15%)
  blocking collectives  205 us (10%)
  local copies, waits for them, and re-layouts  69 us (3%)
  other arithmetic  40.7 us (2%)
    reduce_scatter x1, waiting for transfers between devices, local(): lax.psum_scatter(gate_grad, 'dp', scatter_dimension=0, tiled=True)  196 us
    reduce_scatter x1, waiting for transfers between devices, local(): lax.psum_scatter(up_grad, 'dp', scatter_dimension=0, tiled=True)  196 us
    reduce_scatter x1, waiting for transfers between devices, local(): lax.psum_scatter(down_grad, 'dp', scatter_dimension=1, tiled=True)  112 us
    all_gather x1, waiting for transfers between devices, local(): lax.all_gather(down_weight, 'dp', axis=1, tiled=True)  95.9 us
    reduce_scatter x1, waiting for transfers between devices, local(): lax.psum_scatter(query_weight_grad, 'dp', scatter_dimension=0, tiled=True)  92.3 us
    reduce_scatter x1, waiting for transfers between devices, local(): lax.psum_scatter(value_weight_grad, 'dp', scatter_dimension=0, tiled=True)  92.2 us
    reduce_scatter x1, waiting for transfers between devices, local(): lax.psum_scatter(key_weight_grad, 'dp', scatter_dimension=0, tiled=True)  91.9 us
    reduce_scatter x1, waiting for transfers between devices, local(): lax.psum_scatter(out_weight_grad, 'dp', scatter_dimension=1, tiled=True)  91.6 us
  transfers between devices with their start and end apart: 22, of which 19 were waited for; matrix products, arithmetic and copies ran while one was open for 8% of the time, Pallas kernels for 0%

commit v1 on v0

--- a/solution.py
+++ b/solution.py
@@ -9,6 +9,22 @@
 SEQ = 1024
 EPS = 1e-05
 NEG = -1e30
+
+
+def gather_around(x, axis, dim):
+    ways, here, step = (lax.axis_size(axis), lax.axis_index(axis), x.shape[dim])
+    shape = [n * ways if d == dim else n for d, n in enumerate(x.shape)]
+    full = lax.dynamic_update_slice_in_dim(jnp.zeros(shape, x.dtype), x, here * step, axis=dim)
+    going_up = going_down = x
+    for far in range(1, ways // 2 + 1):
+        going_up = lax.ppermute(going_up, axis, [(d, (d + 1) % ways) for d in range(ways)])
+        full = lax.dynamic_update_slice_in_dim(full, going_up, (here - far) % ways * step, axis=dim)
+        if 2 * far < ways:
+            going_down = lax.ppermute(going_down, axis, [(d, (d - 1) % ways) for d in range(ways)])
+            full = lax.dynamic_update_slice_in_dim(
+                full, going_down, (here + far) % ways * step, axis=dim
+            )
+    return full
 
 
 def rope_angles(positions):
@@ -148,7 +164,7 @@
         lax.all_gather(first_shift, "dp", axis=0, tiled=True),
     )
     gate_full, up_full, down_full, gain_two, shift_two = (
-        lax.all_gather(gate_weight, "dp", axis=0, tiled=True),
+        gather_around(gate_weight, "dp", 0),
         lax.all_gather(up_weight, "dp", axis=0, tiled=True),
         lax.all_gather(down_weight, "dp", axis=1, tiled=True),
         lax.all_gather(second_gain, "dp", axis=0, tiled=True),

time: 2130 us -> 2160 us (1.014)
    ppermute x0 -> x7, waiting for transfers between devices: none -> 113 us  [the longest x4 104 us: gather_around(): lax.ppermute(going_up, axis, [(d, (d + 1) % ways) for d in range(ways)])]
    all_gather x1, waiting for transfers between devices: 95.9 us -> 31.6 us  [local(): lax.all_gather(down_weight, 'dp', axis=1, tiled=True)]
    all_gather x1, waiting for transfers between devices: 22.5 us -> 0.01 us  [local(): grad_full = lax.all_gather(out_grad, 'tensor', axis=0, tiled=True)]
  transfers between devices with their start and end apart: 22 -> 29, of which waited for: 19 -> 23; matrix products, arithmetic and copies ran while one was open for 8% -> 10% of each run, Pallas kernels for 0% -> 0%
where the time goes in v1:
time: 2160 us; the launch traced here: 2150 us
  waiting for transfers between devices  1460 us (68%)
  matrix products  323 us (15%)
  blocking collectives  205 us (9%)
  local copies, waits for them, and re-layouts  82.7 us (4%)
  other arithmetic  40.7 us (2%)
    reduce_scatter x1, waiting for transfers between devices, local(): lax.psum_scatter(gate_grad, 'dp', scatter_dimension=0, tiled=True)  196 us
    reduce_scatter x1, waiting for transfers between devices, local(): lax.psum_scatter(up_grad, 'dp', scatter_dimension=0, tiled=True)  196 us
    reduce_scatter x1, waiting for transfers between devices, local(): lax.psum_scatter(down_grad, 'dp', scatter_dimension=1, tiled=True)  112 us
    ppermute x4, waiting for transfers between devices, gather_around(): lax.ppermute(going_up, axis, [(d, (d + 1) % ways) for d in range(ways)])  104 us
    reduce_scatter x1, waiting for transfers between devices, local(): lax.psum_scatter(query_weight_grad, 'dp', scatter_dimension=0, tiled=True)  92.3 us
    reduce_scatter x1, waiting for transfers between devices, local(): lax.psum_scatter(value_weight_grad, 'dp', scatter_dimension=0, tiled=True)  92.2 us
    reduce_scatter x1, waiting for transfers between devices, local(): lax.psum_scatter(key_weight_grad, 'dp', scatter_dimension=0, tiled=True)  91.9 us
    reduce_scatter x1, waiting for transfers between devices, local(): lax.psum_scatter(out_weight_grad, 'dp', scatter_dimension=1, tiled=True)  91.6 us
  transfers between devices with their start and end apart: 29, of which 23 were waited for; matrix products, arithmetic and copies ran while one was open for 10% of the time, Pallas kernels for 0%

profile of v1, /device:TPU:0, one launch (start us, length us, event | category | flops | bytes accessed | tf_op | source)
XLA Modules:
  0.0 2151.6 jit_solution(16382517630903046264)
XLA Ops:
  9.3 22.2 %all-gather.1 = bf16[8,1,256]{2,1,0:T(2,128)(2,1)S(1)} all-gather(bf16[1,1,256]{2,1,0:T(2,128)(2,1)S(1)} %reshape.335), channel_id=1, replica_groups=mesh['dp'=8,'tensor'=4] {'dp'}, dimensions={0}, use_global_device_ids=true | all-gather | bytes 4608 | tf_op jit(solution)/shard_map/all_gather | solution.py:164
  31.5 16.4 all-gather
  55.4 26.0 %all_gather.65 = bf16[8,64]{0,1:T(8,128)(2,1)S(1)} all-gather(bf16[8,8]{0,1:T(8,128)(2,1)S(1)} %copy.48), channel_id=1, replica_groups=mesh['dp'=8,'tensor'=4] {'dp'}, dimensions={1}, use_global_device_ids=true | all-gather | bytes 1152 | tf_op jit(solution)/shard_map/all_gather | solution.py:162
  81.6 26.0 %all_gather.62 = bf16[8,64]{0,1:T(8,128)(2,1)S(1)} all-gather(bf16[8,8]{0,1:T(8,128)(2,1)S(1)} %copy.46), channel_id=1, replica_groups=mesh['dp'=8,'tensor'=4] {'dp'}, dimensions={1}, use_global_device_ids=true | all-gather | bytes 1152 | tf_op jit(solution)/shard_map/all_gather | solution.py:161
  108.6 5.2 convolution_add_fusion.1
  115.3 33.6 %all-gather.18.cloned.1.call-done = bf16[2048,512]{1,0:T(8,128)(2,1)} async-done(((bf16[256,512]{1,0:T(8,128)(2,1)}), bf16[2048,512]{1,0:T(8,128)(2,1)}) %all-gather.18.cloned.1.call-update) | async-done | bytes 2097168 | tf_op jit(solution)/shard_map/all_gather | solution.py:157
  148.9 5.2 convolution_add_fusion.2
  157.0 41.7 %all-gather.22.cloned.1.call-done = bf16[2048,512]{1,0:T(8,128)(2,1)} async-done(((bf16[256,512]{1,0:T(8,128)(2,1)}), bf16[2048,512]{1,0:T(8,128)(2,1)}) %all-gather.22.cloned.1.call-update) | async-done | bytes 2097168 | tf_op jit(solution)/shard_map/all_gather | solution.py:159
  198.7 6.2 add_convert_fusion.2
  204.9 34.0 %while.31 = (s32[]{:T(128)}, bf16[2,512,8,64]{1,3,2,0:T(8,128)(2,1)S(1)}, f32[2,8,512]{2,1,0:T(8,128)S(1)}, s32[2]{0:T(128)S(1)}, s32[1024]{0:T(1024)S(1)}, /*in...) while((s32[]{:T(128)}, ...), condition=%wide.region_5.6_spmd, body=%wide.region_2.5_spmd.sunk | while | flops 1125643776 | bytes 56252800 | solution.py:96
  216.1 5.9 fusion.147
  233.0 5.9 fusion.147
  240.2 10.0 all-gather.24.cloned.1.call-done
  250.2 7.2 fusion.66
  259.8 17.7 all-gather.3
  277.5 16.9 all-gather.2
  294.4 33.1 %reduce-scatter.14.cloned.1.call-done = f32[256,2048]{1,0:T(8,128)} async-done(((f32[1024,2048]{1,0:T(8,128)}), f32[256,2048]{1,0:T(8,128)}) %reduce-scatter.14.cloned.1.call-update) | async-done | bytes 2097168 | tf_op jit(solution)/shard_map/reduce_scatter | solution.py:195
  336.1 27.9 %collective-permute-done = bf16[256,1408]{1,0:T(8,128)(2,1)} collective-permute-done((bf16[256,1408]{1,0:T(8,128)(2,1)}, bf16[256,1408]{1,0:T(8,128)(2,1)}, u32[]{:S(2)}, u32[]{:S(2)}) %collective-permute-start) | collective-permute-done | bytes 720928 | tf_op jit(solution)/shard_map/ppermute | solution.py:20
  374.5 30.0 %collective-permute-done.2 = bf16[256,1408]{1,0:T(8,128)(2,1)S(1)} collective-permute-done((bf16[256,1408]{1,0:T(8,128)(2,1)}, bf16[256,1408]{1,0:T(8,128)(2,1)S(1)}, u32[]{:S(2)}, u32[]{:S(2)}) %collective-permute-start.2) | collective-permute-done | bytes 720928 | tf_op jit(solution)/shard_map/ppermute | solution.py:20
  414.9 22.4 %collective-permute-done.4 = bf16[256,1408]{1,0:T(8,128)(2,1)S(1)} collective-permute-done((bf16[256,1408]{1,0:T(8,128)(2,1)S(1)}, bf16[256,1408]{1,0:T(8,128)(2,1)S(1)}, u32[]{:S(2)}, u32[]{:S(2)}) %collective-permute-start.4) | collective-permute-done | bytes 720928 | tf_op jit(solution)/shard_map/ppermute | solution.py:20
  440.5 8.8 collective-permute-done.5
  450.2 23.6 %collective-permute-done.6 = bf16[256,1408]{1,0:T(8,128)(2,1)S(1)} collective-permute-done((bf16[256,1408]{1,0:T(8,128)(2,1)S(1)}, bf16[256,1408]{1,0:T(8,128)(2,1)S(1)}, u32[]{:S(2)}, u32[]{:S(2)}) %collective-permute-start.6) | collective-permute-done | bytes 720928 | tf_op jit(solution)/shard_map/ppermute | solution.py:20
  474.8 31.6 %all-gather.30.cloned.1.call-done = bf16[1408,2048]{1,0:T(8,128)(2,1)} async-done(((bf16[1408,256]{1,0:T(8,128)(2,1)}), bf16[1408,2048]{1,0:T(8,128)(2,1)}) %all-gather.30.cloned.1.call-update) | async-done | bytes 5767184 | tf_op jit(solution)/shard_map/all_gather | solution.py:169
  506.4 11.8 fusion.68
  518.1 81.4 %all-gather.28.cloned.1.call-done = bf16[2048,1408]{1,0:T(8,128)(2,1)} async-done(((bf16[256,1408]{1,0:T(8,128)(2,1)}), bf16[2048,1408]{1,0:T(8,128)(2,1)}) %all-gather.28.cloned.1.call-update) | async-done | bytes 5767184 | tf_op jit(solution)/shard_map/all_gather | solution.py:168
  599.5 34.8 %all-gather.26.cloned.1.call-done = bf16[1024,2048]{1,0:T(8,128)(2,1)} async-done(((bf16[256,2048]{1,0:T(8,128)(2,1)}), bf16[1024,2048]{1,0:T(8,128)(2,1)}) %all-gather.26.cloned.1.call-update) | async-done | bytes 4194320 | tf_op jit(solution)/shard_map/all_gather | solution.py:203
  634.3 11.0 fusion.67
  645.3 13.8 multiply_convert_fusion.1
  659.1 70.3 %all-gather.34.cloned.1.call-done = bf16[2048,1408]{1,0:T(8,128)(2,1)} async-done(((bf16[256,1408]{1,0:T(8,128)(2,1)}), bf16[2048,1408]{1,0:T(8,128)(2,1)}) %all-gather.34.cloned.1.call-update) | async-done | bytes 5767184 | tf_op jit(solution)/shard_map/all_gather | solution.py:223
  729.4 9.7 fusion.69
  739.1 9.3 convolution_add_fusion
  748.5 10.9 convolution_convert_fusion
  759.5 59.0 %reduce-scatter.18.cloned.1.call-done = f32[256,2048]{1,0:T(8,128)} async-done(((f32[1024,2048]{1,0:T(8,128)}), f32[256,2048]{1,0:T(8,128)}) %reduce-scatter.18.cloned.1.call-update) | async-done | bytes 2097168 | tf_op jit(solution)/shard_map/reduce_scatter | solution.py:236
  821.6 44.0 %reduce-scatter.16.cloned.1.call-done = bf16[256,2048]{1,0:T(8,128)(2,1)} async-done(((bf16[1024,2048]{1,0:T(8,128)(2,1)}), bf16[256,2048]{1,0:T(8,128)(2,1)}) %reduce-scatter.16.cloned.1.call-update) | async-done | bytes 1048592 | tf_op jit(solution)/shard_map/reduce_scatter | solution.py:211
  870.6 34.6 %all-gather.36.cloned.1.call-done = bf16[1024,2048]{1,0:T(8,128)(2,1)} async-done(((bf16[256,2048]{1,0:T(8,128)(2,1)}), bf16[1024,2048]{1,0:T(8,128)(2,1)}) %all-gather.36.cloned.1.call-update) | async-done | bytes 4194320 | tf_op jit(solution)/shard_map/all_gather | solution.py:248
  905.2 6.2 convolution_convert_fusion.1
  911.4 183.1 %while.32 = (s32[]{:T(128)}, f32[1024,8,64]{0,2,1:T(8,128)}, f32[1024,8,64]{0,2,1:T(8,128)S(1)}, f32[2,512,8,64]{1,0,3,2:T(2,128)}, s32[2]{0:T(128)S(1)}, /*inde...) while((s32[]{:T(128)}, f32[1024,8,64]{0,2,1:T(8,128)}, ...), condition=%wide.region_15.16_spmd.clone, body=%wide.region_13.15_spmd.clone.sunk | while | flops 2746756608 | bytes 238098896 | solution.py:128
  913.4 5.9 subtract_exponential_fusion.3
  925.1 9.5 fusion.158
  934.6 22.9 %fusion.159 = f32[1,512,8,64]{1,3,2,0:T(8,128)} fusion(bf16[1024,8,64]{0,2,1:T(8,128)(2,1)} %get-tuple-element.590, f32[8,512,1024]{2,1,0:T(8,128)} %copy-done, f32[8,512,1024]{2,1,0:T(8,128)} %fusion.158), kind=kOutput, calls=%fused_computation.31.clone.1 | convolution fusion | flops 557847552 | bytes 35651584 | tf_op jit(solution)/shard_map/while/body/eval_jaxpr/hqk,khd->qhd/dot_general | solution.py:116
  957.5 23.5 %bitcast_add_fusion.4 = f32[1024,8,64]{0,2,1:T(8,128)} fusion(f32[1024,8,64]{0,2,1:T(8,128)} %get-tuple-element.566, f32[8,512,1024]{2,1,0:T(8,128)} %copy-done, f32[8,512,1024]{2,1,0:T(8,128)} %fusion.158, pred[]{:T(512)S(6)} %compare.21, bf16[1024,8,64]{0,2,1:T(8,128)(2,1)} %get-tuple-element.588, s32[]{:T(128)S(6)} %select_n.144), kind=kOutput, calls=%fused_computation.29.clone.1 | convolution fusion | flops 558896128 | bytes 71827464 | tf_op jit(solution)/shard_map/while/body/eval_jaxpr/hqk,qhd->khd/dot_general | solution.py:117
  983.2 19.5 dynamic_update_slice.68
  1004.5 5.9 subtract_exponential_fusion.3
  1016.2 9.5 fusion.158
  1025.7 22.9 %fusion.159 = f32[1,512,8,64]{1,3,2,0:T(8,128)} fusion(bf16[1024,8,64]{0,2,1:T(8,128)(2,1)} %get-tuple-element.590, f32[8,512,1024]{2,1,0:T(8,128)} %copy-done, f32[8,512,1024]{2,1,0:T(8,128)} %fusion.158), kind=kOutput, calls=%fused_computation.31.clone.1 | convolution fusion | flops 557847552 | bytes 35651584 | tf_op jit(solution)/shard_map/while/body/eval_jaxpr/hqk,khd->qhd/dot_general | solution.py:116
  1048.6 24.0 %bitcast_add_fusion.4 = f32[1024,8,64]{0,2,1:T(8,128)} fusion(f32[1024,8,64]{0,2,1:T(8,128)} %get-tuple-element.566, f32[8,512,1024]{2,1,0:T(8,128)} %copy-done, f32[8,512,1024]{2,1,0:T(8,128)} %fusion.158, pred[]{:T(512)S(6)} %compare.21, bf16[1024,8,64]{0,2,1:T(8,128)(2,1)} %get-tuple-element.588, s32[]{:T(128)S(6)} %select_n.144), kind=kOutput, calls=%fused_computation.29.clone.1 | convolution fusion | flops 558896128 | bytes 71827464 | tf_op jit(solution)/shard_map/while/body/eval_jaxpr/hqk,qhd->khd/dot_general | solution.py:117
  1074.8 19.5 dynamic_update_slice.68
  1109.1 5.8 add_add_fusion
  1115.0 12.3 fusion.78
  1127.3 13.0 fusion.77
  1140.4 11.9 fusion.76
  1152.3 7.0 fusion.75
  1159.4 6.7 fusion.74
  1166.4 6.6 fusion.73
  1173.0 6.6 fusion.72
  1183.3 38.5 %all-reduce.8 = (f32[8,64]{1,0:T(8,128)S(1)}, f32[8,16]{1,0:T(8,128)}, f32[8,64]{1,0:T(8,128)S(1)}) all-reduce(f32[8,64]{1,0:T(8,128)S(1)} %fusion.61, f32[8,16]{1,0:T(8,128)S(1)} %bitcast.138, f32[8,64]{1,0:T(8,128)S(1)} %get-tuple-element.370), channel_id=11, replica_groups=mesh['dp'=8,'tensor'=4] {'dp'}, use_global_device_ids=true, to_apply=%region_27.28.clone | all-reduce | flops 1152 | bytes 9216
  1225.9 41.1 %all-reduce.7 = (f32[2048]{0:T(1024)S(1)}, f32[2048]{0:T(1024)S(1)}, f32[2048]{0:T(1024)S(1)}, f32[2048]{0:T(1024)S(1)}) all-reduce(f32[2048]{0:T(1024)S(1)} %get-tuple-element.302, f32[2048]{0:T(1024)S(1)} %get-tuple-element.307, f32[2048]{0:T(1024)S(1)} %copy-done.24, ...), channel_id=6, replica_groups=mesh['dp'=8,'tensor'=4] {'dp','tensor'}, use_global_device_ids=true, to_apply=%region_20.21.clone | all-reduce | flops 8192 | bytes 65536
  1273.1 111.9 %reduce-scatter.34.cloned.1.call-done = f32[1408,256]{1,0:T(8,128)} async-done(((f32[1408,2048]{1,0:T(8,128)}), f32[1408,256]{1,0:T(8,128)}) %reduce-scatter.34.cloned.1.call-update) | async-done | bytes 1441808 | tf_op jit(solution)/shard_map/reduce_scatter | solution.py:286
  1385.0 195.8 %reduce-scatter.32.cloned.1.call-done = f32[256,1408]{1,0:T(8,128)} async-done(((f32[2048,1408]{1,0:T(8,128)}), f32[256,1408]{1,0:T(8,128)}) %reduce-scatter.32.cloned.1.call-update) | async-done | bytes 1441808 | tf_op jit(solution)/shard_map/reduce_scatter | solution.py:285
  1580.8 195.8 %reduce-scatter.30.cloned.1.call-done = f32[256,1408]{1,0:T(8,128)} async-done(((f32[2048,1408]{1,0:T(8,128)}), f32[256,1408]{1,0:T(8,128)}) %reduce-scatter.30.cloned.1.call-update) | async-done | bytes 1441808 | tf_op jit(solution)/shard_map/reduce_scatter | solution.py:284
  1776.6 91.6 %reduce-scatter.28.cloned.1.call-done = f32[512,256]{1,0:T(8,128)} async-done(((f32[512,2048]{1,0:T(8,128)}), f32[512,256]{1,0:T(8,128)}) %reduce-scatter.28.cloned.1.call-update) | async-done | bytes 524304 | tf_op jit(solution)/shard_map/reduce_scatter | solution.py:292
  1868.2 92.2 %reduce-scatter.26.cloned.1.call-done = f32[256,512]{1,0:T(8,128)} async-done(((f32[2048,512]{1,0:T(8,128)}), f32[256,512]{1,0:T(8,128)}) %reduce-scatter.26.cloned.1.call-update) | async-done | bytes 524304 | tf_op jit(solution)/shard_map/reduce_scatter | solution.py:291
  1960.4 91.9 %reduce-scatter.24.cloned.1.call-done = f32[256,512]{1,0:T(8,128)} async-done(((f32[2048,512]{1,0:T(8,128)}), f32[256,512]{1,0:T(8,128)}) %reduce-scatter.24.cloned.1.call-update) | async-done | bytes 524304 | tf_op jit(solution)/shard_map/reduce_scatter | solution.py:290
  2052.3 92.3 %reduce-scatter.22.cloned.1.call-done = f32[256,512]{1,0:T(8,128)} async-done(((f32[2048,512]{1,0:T(8,128)}), f32[256,512]{1,0:T(8,128)}) %reduce-scatter.22.cloned.1.call-update) | async-done | bytes 524304 | tf_op jit(solution)/shard_map/reduce_scatter | solution.py:289
  (254 shorter events, 128.0 us)
Async XLA Ops:
  7.2 44.5 %copy-start.1 = (bf16[256,2048]{1,0:T(8,128)(2,1)S(1)}, bf16[256,2048]{1,0:T(8,128)(2,1)}, u32[]{:S(2)}) copy-start(bf16[256,2048]{1,0:T(8,128)(2,1)} %param.22) | copy-start | bytes 3145732
  7.2 101.4 %all-gather.20.cloned.1.call-start = ((), (), s32[]{:S(2)}) async-start(), calls=%async_computation.13 | async-start | bytes 2359296 | tf_op jit(solution)/shard_map/all_gather | solution.py:158
  7.9 100.6 %all-gather.16.cloned.1.call-start = ((), (), s32[]{:S(2)}) async-start(), calls=%async_computation.11 | async-start | bytes 5242880 | tf_op jit(solution)/shard_map/all_gather | solution.py:176
  48.0 3.2 copy-start.22
  48.0 7.2 copy-start.32
  48.0 7.3 copy-start.33
  48.0 7.3 copy-start.30
  48.0 7.3 copy-start.31
  53.2 95.7 %all-gather.18.cloned.1.call-start = ((), (), s32[]{:S(2)}) async-start(), calls=%async_computation.12 | async-start | bytes 2359296 | tf_op jit(solution)/shard_map/all_gather | solution.py:157
  53.9 144.8 %all-gather.22.cloned.1.call-start = ((), (), s32[]{:S(2)}) async-start(), calls=%async_computation.14 | async-start | bytes 2359296 | tf_op jit(solution)/shard_map/all_gather | solution.py:159
  54.5 195.7 %all-gather.24.cloned.1.call-start = ((), (), s32[]{:S(2)}) async-start(), calls=%async_computation.15 | async-start | bytes 2359296 | tf_op jit(solution)/shard_map/all_gather | solution.py:160
  55.1 272.5 %reduce-scatter.14.cloned.1.call-start = ((), (), s32[]{:S(2)}) async-start(), calls=%async_computation.16 | async-start | bytes 10485760 | tf_op jit(solution)/shard_map/reduce_scatter | solution.py:195
  108.6 45.7 %copy-start.19 = (f32[1024,8]{0,1:T(8,128)}, f32[1024,8]{0,1:T(8,128)S(1)}, u32[]{:S(2)}) copy-start(f32[1024,8]{0,1:T(8,128)S(1)} %get-tuple-element.379) | copy-start | bytes 98308
  157.0 47.9 %copy-start.17 = (s32[1024]{0:T(1024)S(1)}, s32[1024]{0:T(1024)}, u32[]{:S(2)}) copy-start(s32[1024]{0:T(1024)} %param.23) | copy-start | bytes 12292
  240.2 17.2 copy-start.16
  257.5 2.3 copy-start.38
  257.5 2.3 copy-start.39
  257.5 70.1 %copy-start.2 = (bf16[256,2048]{1,0:T(8,128)(2,1)S(1)}, bf16[256,2048]{1,0:T(8,128)(2,1)}, u32[]{:S(2)}) copy-start(bf16[256,2048]{1,0:T(8,128)(2,1)} %param.22) | copy-start | bytes 3145732
  257.5 217.3 %all-gather.32.cloned.1.call-start = ((), (), s32[]{:S(2)}) async-start(), calls=%async_computation.21 | async-start | bytes 5242880 | tf_op jit(solution)/shard_map/all_gather | solution.py:229
  258.3 248.1 %all-gather.30.cloned.1.call-start = ((), (), s32[]{:S(2)}) async-start(), calls=%async_computation.19 | async-start | bytes 6488064 | tf_op jit(solution)/shard_map/all_gather | solution.py:169
  259.0 340.5 %all-gather.28.cloned.1.call-start = ((), (), s32[]{:S(2)}) async-start(), calls=%async_computation.18 | async-start | bytes 6488064 | tf_op jit(solution)/shard_map/all_gather | solution.py:168
  259.7 374.5 %all-gather.26.cloned.1.call-start = ((), (), s32[]{:S(2)}) async-start(), calls=%async_computation.17 | async-start | bytes 5242880 | tf_op jit(solution)/shard_map/all_gather | solution.py:203
  331.3 398.1 %all-gather.34.cloned.1.call-start = ((), (), s32[]{:S(2)}) async-start(), calls=%async_computation.22 | async-start | bytes 6488064 | tf_op jit(solution)/shard_map/all_gather | solution.py:223
  331.3 32.7 %collective-permute-start = (bf16[256,1408]{1,0:T(8,128)(2,1)}, bf16[256,1408]{1,0:T(8,128)(2,1)}, u32[]{:S(2)}, u32[]{:S(2)}) collective-permute-start(bf16[256,1408]{1,0:T(8,128)(2,1)} %param.36), channel_id=1, source_target_pairs={{0,4},{4,8},{8,12},{12,16},{16,20},{20,24},{24,28},{28,0},{1,5},{5... | collective-permute-start | bytes 2162696 | tf_op jit(solution)/shard_map/ppermute | solution.py:20
  332.8 33.8 %collective-permute-start.1 = (bf16[256,1408]{1,0:T(8,128)(2,1)}, bf16[256,1408]{1,0:T(8,128)(2,1)}, u32[]{:S(2)}, u32[]{:S(2)}) collective-permute-start(bf16[256,1408]{1,0:T(8,128)(2,1)} %param.36), channel_id=1, source_target_pairs={{0,28},{4,0},{8,4},{12,8},{16,12},{20,16},{24,20},{28,24},{1,29},{... | collective-permute-start | bytes 2162696 | tf_op jit(solution)/shard_map/ppermute | solution.py:23
  364.0 40.5 %collective-permute-start.2 = (bf16[256,1408]{1,0:T(8,128)(2,1)}, bf16[256,1408]{1,0:T(8,128)(2,1)S(1)}, u32[]{:S(2)}, u32[]{:S(2)}) collective-permute-start(bf16[256,1408]{1,0:T(8,128)(2,1)} %collective-permute-done), channel_id=1, source_target_pairs={{0,4},{4,8},{8,12},{12,16},{16,20},{20,24},{24,28},{28,0},{1,5},{5... | collective-permute-start | bytes 2162696 | tf_op jit(solution)/shard_map/ppermute | solution.py:20
  366.5 452.0 %reduce-scatter.18.cloned.1.call-start = ((), (), s32[]{:S(2)}) async-start(), calls=%async_computation.23 | async-start | bytes 10485760 | tf_op jit(solution)/shard_map/reduce_scatter | solution.py:236
  366.7 44.3 %collective-permute-start.3 = (bf16[256,1408]{1,0:T(8,128)(2,1)}, bf16[256,1408]{1,0:T(8,128)(2,1)S(1)}, u32[]{:S(2)}, u32[]{:S(2)}) collective-permute-start(bf16[256,1408]{1,0:T(8,128)(2,1)} %collective-permute-done.1), channel_id=1, source_target_pairs={{0,28},{4,0},{8,4},{12,8},{16,12},{20,16},{24,20},{28,24},{1,29},{... | collective-permute-start | bytes 2162696 | tf_op jit(solution)/shard_map/ppermute | solution.py:23
  404.5 32.9 %collective-permute-start.4 = (bf16[256,1408]{1,0:T(8,128)(2,1)S(1)}, bf16[256,1408]{1,0:T(8,128)(2,1)S(1)}, u32[]{:S(2)}, u32[]{:S(2)}) collective-permute-start(bf16[256,1408]{1,0:T(8,128)(2,1)S(1)} %collective-permute-done.2), channel_id=1, source_target_pairs={{0,4},{4,8},{8,12},{12,16},{16,20},{20,24},{24,28},{28,0},{1,5},{5... | collective-permute-start | bytes 2162696 | tf_op jit(solution)/shard_map/ppermute | solution.py:20
  411.0 38.3 %collective-permute-start.5 = (bf16[256,1408]{1,0:T(8,128)(2,1)S(1)}, bf16[256,1408]{1,0:T(8,128)(2,1)S(1)}, u32[]{:S(2)}, u32[]{:S(2)}) collective-permute-start(bf16[256,1408]{1,0:T(8,128)(2,1)S(1)} %collective-permute-done.3), channel_id=1, source_target_pairs={{0,28},{4,0},{8,4},{12,8},{16,12},{20,16},{24,20},{28,24},{1,29},{... | collective-permute-start | bytes 2162696 | tf_op jit(solution)/shard_map/ppermute | solution.py:23
  437.4 36.5 %collective-permute-start.6 = (bf16[256,1408]{1,0:T(8,128)(2,1)S(1)}, bf16[256,1408]{1,0:T(8,128)(2,1)S(1)}, u32[]{:S(2)}, u32[]{:S(2)}) collective-permute-start(bf16[256,1408]{1,0:T(8,128)(2,1)S(1)} %collective-permute-done.4), channel_id=1, source_target_pairs={{0,4},{4,8},{8,12},{12,16},{16,20},{20,24},{24,28},{28,0},{1,5},{5... | collective-permute-start | bytes 2162696 | tf_op jit(solution)/shard_map/ppermute | solution.py:20
  634.3 11.0 copy-start.35
  634.3 11.1 copy-start.41
  729.3 9.8 copy-start.34
  729.4 9.8 copy-start.42
  748.5 117.1 %reduce-scatter.16.cloned.1.call-start = ((), (), s32[]{:S(2)}) async-start(), calls=%async_computation.20 | async-start | bytes 5242880 | tf_op jit(solution)/shard_map/reduce_scatter | solution.py:211
  759.5 106.1 %copy-start.8 = (bf16[256,2048]{1,0:T(8,128)(2,1)S(1)}, bf16[256,2048]{1,0:T(8,128)(2,1)}, u32[]{:S(2)}) copy-start(bf16[256,2048]{1,0:T(8,128)(2,1)} %param.39) | copy-start | bytes 3145732
  759.5 145.7 %all-gather.36.cloned.1.call-start = ((), (), s32[]{:S(2)}) async-start(), calls=%async_computation.24 | async-start | bytes 5242880 | tf_op jit(solution)/shard_map/all_gather | solution.py:248
  870.6 352.6 %reduce-scatter.20.cloned.1.call-start = ((), (), s32[]{:S(2)}) async-start(), calls=%async_computation.25 | async-start | bytes 10485760 | tf_op jit(solution)/shard_map/reduce_scatter | solution.py:274
  919.3 5.8 copy-start
  1010.5 5.8 copy-start
  1098.5 2.1 copy-start.15
  1098.5 2.2 copy-start.20
  1098.5 2.3 copy-start.21
  1100.2 3.0 copy-start.4
  1100.8 2.0 copy-start.6
  1104.2 2.4 copy-start.37
  1106.7 2.4 copy-start.14
  1114.9 270.0 %reduce-scatter.34.cloned.1.call-start = ((), (), s32[]{:S(2)}) async-start(), calls=%async_computation.32 | async-start | bytes 12976128 | tf_op jit(solution)/shard_map/reduce_scatter | solution.py:286
  1127.3 453.5 %reduce-scatter.32.cloned.1.call-start = ((), (), s32[]{:S(2)}) async-start(), calls=%async_computation.31 | async-start | bytes 12976128 | tf_op jit(solution)/shard_map/reduce_scatter | solution.py:285
  1140.3 636.3 %reduce-scatter.30.cloned.1.call-start = ((), (), s32[]{:S(2)}) async-start(), calls=%async_computation.30 | async-start | bytes 12976128 | tf_op jit(solution)/shard_map/reduce_scatter | solution.py:284
  1152.3 715.9 %reduce-scatter.28.cloned.1.call-start = ((), (), s32[]{:S(2)}) async-start(), calls=%async_computation.29 | async-start | bytes 4718592 | tf_op jit(solution)/shard_map/reduce_scatter | solution.py:292
  1159.4 801.0 %reduce-scatter.26.cloned.1.call-start = ((), (), s32[]{:S(2)}) async-start(), calls=%async_computation.28 | async-start | bytes 4718592 | tf_op jit(solution)/shard_map/reduce_scatter | solution.py:291
  1166.2 886.1 %reduce-scatter.24.cloned.1.call-start = ((), (), s32[]{:S(2)}) async-start(), calls=%async_computation.27 | async-start | bytes 4718592 | tf_op jit(solution)/shard_map/reduce_scatter | solution.py:290
  1173.0 971.6 %reduce-scatter.22.cloned.1.call-start = ((), (), s32[]{:S(2)}) async-start(), calls=%async_computation.26 | async-start | bytes 4718592 | tf_op jit(solution)/shard_map/reduce_scatter | solution.py:289
  1179.6 3.5 copy-start.5
  1179.6 3.5 copy-start.10
  1179.6 43.5 %copy-start.3 = (bf16[256,2048]{1,0:T(8,128)(2,1)S(1)}, bf16[256,2048]{1,0:T(8,128)(2,1)}, u32[]{:S(2)}) copy-start(bf16[256,2048]{1,0:T(8,128)(2,1)} %param.22) | copy-start | bytes 3145732
  1179.6 43.5 %copy-start.23 = (f32[8,1,256]{2,1,0:T(1,128)S(1)}, f32[8,1,256]{2,1,0:T(1,128)}, u32[]{:S(2)}) copy-start(f32[8,1,256]{2,1,0:T(1,128)} %copy-done.22) | copy-start | bytes 24580
  1179.7 43.5 %copy-start.27 = (f32[256]{0:T(256)S(1)}, f32[256]{0:T(256)}, u32[]{:S(2)}) copy-start(f32[256]{0:T(256)} %copy-done.26) | copy-start | bytes 3076
  1179.7 43.5 %copy-start.29 = (f32[256]{0:T(256)S(1)}, f32[256]{0:T(256)}, u32[]{:S(2)}) copy-start(f32[256]{0:T(256)} %copy-done.28) | copy-start | bytes 3076
  1183.1 42.8 %copy-start.24 = (f32[2048]{0:T(1024)S(1)}, f32[2048]{0:T(1024)}, u32[]{:S(2)}) copy-start(f32[2048]{0:T(1024)} %get-tuple-element.300) | copy-start | bytes 24580
  1183.1 42.8 %copy-start.25 = (f32[2048]{0:T(1024)S(1)}, f32[2048]{0:T(1024)}, u32[]{:S(2)}) copy-start(f32[2048]{0:T(1024)} %get-tuple-element.306) | copy-start | bytes 24580
  1223.2 46.1 %copy-start.7 = (f32[256,2048]{1,0:T(8,128)S(1)}, f32[256,2048]{1,0:T(8,128)}, u32[]{:S(2)}) copy-start(f32[256,2048]{1,0:T(8,128)} %reduce-scatter.20.cloned.1.call-done) | copy-start | bytes 6291460
  (9 other events, 10.2 us)
Sparse Core Ops, SparseCore 0:
  10.2 52.0 all-gather.19
  64.4 33.0 all-gather.15
  99.6 49.2 all-gather.17
  150.9 47.7 all-gather.21
  200.6 49.5 all-gather.23
  257.6 69.8 reduce-scatter.13
  329.2 34.4 all-gather.31
  365.9 140.3 all-gather.29
  508.8 90.6 all-gather.27
  601.5 32.6 all-gather.25
  636.7 92.6 all-gather.33
  748.6 69.8 reduce-scatter.17
  821.0 44.4 reduce-scatter.15
  870.7 34.4 all-gather.35
  1115.0 71.6 reduce-scatter.19
  1190.8 194.0 reduce-scatter.33
  1389.0 191.7 reduce-scatter.31
  1584.8 191.7 reduce-scatter.29
  1780.8 87.3 reduce-scatter.27
  1872.7 87.6 reduce-scatter.25
  1964.6 87.6 reduce-scatter.23
  2056.9 87.6 reduce-scatter.21
